TPU v7x, 256 devices: a whole 4x4x8 slice. The times are simulated.
256 devices in a mesh: row: 16 (over y, z_lo), col: 16 (over z_hi, x, core).
Axes of the slice: x: 4, y: 4, z: 8 (z_hi: 2, z_lo: 4; z = z_hi * 4 + z_lo), core: 2. Of those that a mesh axis runs over, the one named last changes fastest.
Arguments:
- start_vectors: float32 [64, 32768], P(None, ('row', 'col')), may hold values from -6 to 6
- cluster_order: int32 [256, 128], P(('row', 'col')), may hold values from 0 to 127, each once within a row
- weights: bfloat16 [32768, 16, 2048], P('row', 'col'), may hold values from 0 to 1, as said below
- block_mask: int32 [256, 16, 16], P('row', 'col'), may hold values 0 or 1
Outputs:
- embedding: float32 [64, 32768], P(None, ('row', 'col'))
Inputs may be any that keep to these rules, and one draw needn't show every extreme that they name: Each row of cluster_order holds every number of 0 to 127 once. `block_mask`: entries below the diagonal blocks are read only through their mirror. `weights`: every node except the last of its cluster block has a positive weight to the next node of its cluster block.
All inputs are finite; a program needn't handle non-finite values.
Results may differ from a plain program's by a relative error of at most 0.00087.
Values may be sent and summed in bfloat16 or wider, within the bound.
A program may use at most 64 MiB of HBM per device.

v0:
```python
import math
import jax
import jax.numpy as jnp
from jax import lax
from jax.sharding import PartitionSpec as P

ITERS = 3


def orthonormalize(panel_in):
    partial_gram = lax.dot_general(
        panel_in,
        panel_in,
        (((1,), (1,)), ((), ())),
        precision=lax.Precision.HIGHEST,
        preferred_element_type=jnp.float32,
    )
    total_gram = lax.psum(partial_gram, ("row", "col"))
    factor = jnp.linalg.cholesky(total_gram)
    return jax.scipy.linalg.solve_triangular(factor, panel_in, lower=True)


def collect_direct(term):
    return lax.psum_scatter(term, "col", scatter_dimension=1, tiled=True)


def direct_part(matrix, vectors):
    return lax.dot_general(
        lax.all_gather(vectors, "row", axis=1, tiled=True),
        matrix,
        (((1,), (1,)), ((), ())),
        preferred_element_type=jnp.float32,
    )


def local(start_vectors, cluster_order, weights, block_mask):
    row_index = lax.axis_index("row")
    col_index = lax.axis_index("col")
    row_count = lax.axis_size("row")
    col_count = lax.axis_size("col")
    block_len = start_vectors.shape[1]
    stored = weights[:, 0, :]
    live_mask = block_mask[:, 0, :]
    local_rows = row_index * col_count * block_len + jnp.arange(
        col_count * block_len, dtype=jnp.int32
    )
    col_position = jnp.arange(row_count * block_len, dtype=jnp.int32)
    local_cols = (
        col_position // block_len * col_count + col_index
    ) * block_len + col_position % block_len
    row_spans = row_index * col_count + jnp.arange(col_count, dtype=jnp.int32)
    col_spans = jnp.arange(row_count, dtype=jnp.int32) * col_count + col_index
    same_block = row_spans[:, None] == col_spans[None, :]
    keep_upper = ((live_mask > 0) | same_block)[:, None, :, None] & (
        local_rows.reshape(col_count, block_len, 1, 1)
        < local_cols.reshape(1, 1, row_count, block_len)
    )
    zero_value = jnp.zeros((), jnp.bfloat16)
    upper_part = jnp.where(
        keep_upper, stored.reshape(col_count, block_len, row_count, block_len), zero_value
    )
    ones_cols = jnp.ones((row_count * block_len,), jnp.bfloat16)
    matrix = upper_part.reshape(col_count * block_len, row_count * block_len)
    ones_rows = jnp.ones((col_count * block_len,), jnp.bfloat16)

    def mirror_sums(term):
        return lax.psum_scatter(term, "row", scatter_dimension=1, tiled=True)

    row_totals = jnp.dot(matrix, ones_cols, preferred_element_type=jnp.float32)[None, :]
    col_totals = jnp.dot(ones_rows, matrix, preferred_element_type=jnp.float32)[None, :]
    degree = collect_direct(row_totals) + mirror_sums(col_totals)
    inverse_root = 1.0 / jnp.sqrt(degree)
    picked = jnp.take_along_axis(
        start_vectors, jnp.broadcast_to(cluster_order, start_vectors.shape), axis=1
    )
    panel_now = orthonormalize(picked)
    for round_index in range(ITERS):
        vectors = (inverse_root * panel_now).astype(jnp.bfloat16)
        panel_now = orthonormalize(
            panel_now
            + inverse_root
            * (
                collect_direct(direct_part(matrix, vectors))
                + mirror_sums(
                    jnp.dot(
                        lax.all_gather(vectors, "col", axis=1, tiled=True),
                        matrix,
                        preferred_element_type=jnp.float32,
                    )
                )
            )
        )
    total_nodes = block_len * row_count * col_count
    return math.sqrt(total_nodes) * panel_now


def solution(mesh):
    placed = (
        P(None, ("row", "col")),
        P(("row", "col"), None),
        P("row", "col", None),
        P("row", "col", None),
    )
    return jax.shard_map(
        local, mesh=mesh, in_specs=placed, out_specs=P(None, ("row", "col")), check_vma=False
    )
```

profile of v0, /device:TPU:1, one launch (start us, length us, event | category | flops | bytes accessed | tf_op | source)
XLA Modules:
  0.0 1080.2 jit_solution(14854760492870772984)
XLA Ops:
  6.5 0.7 broadcast_compare_fusion
  7.3 0.1 bitcast_or_fusion
  7.4 1.1 and.66
  8.5 7.7 fusion
  16.3 3.2 copy-done.1
  19.5 3.4 convolution_bitcast_fusion.1
  23.0 7.7 convolution_bitcast_fusion
  30.9 50.7 %gather_fusion = f32[8192]{0:T(1024)S(1)} fusion(f32[64,128]{1,0:T(8,128)S(1)} %copy-done, s32[8192]{0:T(1024)S(1)} %or_bitcast_fusion), kind=kCustom, calls=%fused_computation | custom fusion | bytes 131072 | tf_op jit(solution)/shard_map/jit(take_along_axis)/gather | solution.py:73
  81.5 0.2 fusion.16
  81.7 82.8 %psum.28 = f32[64,64]{0,1:T(8,128)S(1)} all-reduce(f32[64,64]{0,1:T(8,128)S(1)} %fusion.16), channel_id=1, replica_groups=mesh['row'=16,'col'=16] {'row','col'}, use_global_device_ids=true, to_apply=%region_0.1 | all-reduce | flops 4096 | bytes 32768 | tf_op jit(solution)/shard_map/psum | solution.py:18
  164.6 0.1 copy.22
  164.7 5.8 cholesky.74
  170.5 0.6 compare_reduce_fusion.3
  171.2 0.7 fusion.1
  171.8 4.9 custom-call.10
  176.8 0.9 copy.34
  177.7 4.9 reduce-scatter.27.cloned.1.call-done
  182.5 0.9 copy.36
  183.4 0.3 multiply_convert_fusion.2
  183.7 32.5 %all_gather.18 = bf16[64,2048]{1,0:T(8,128)(2,1)S(1)} all-gather(bf16[64,128]{1,0:T(8,128)(2,1)S(1)} %get-tuple-element.6), channel_id=1, replica_groups=mesh['row'=16,'col'=16] {'row'}, dimensions={1}, use_global_device_ids=true | all-gather | bytes 278528 | tf_op jit(solution)/shard_map/all_gather | solution.py:29
  216.2 6.9 fusion.59
  223.1 50.3 %all_gather.19 = bf16[64,2048]{1,0:T(8,128)(2,1)S(1)} all-gather(bf16[64,128]{1,0:T(8,128)(2,1)S(1)} %get-tuple-element.6), channel_id=1, replica_groups=mesh['row'=16,'col'=16] {'col'}, dimensions={1}, use_global_device_ids=true | all-gather | bytes 278528 | tf_op jit(solution)/shard_map/all_gather | solution.py:86
  273.5 5.8 fusion.60
  279.4 35.2 %reduce-scatter.13.cloned.1.call-done = f32[64,128]{1,0:T(8,128)} async-done(((f32[64,2048]{1,0:T(8,128)}), f32[64,128]{1,0:T(8,128)}) %reduce-scatter.13.cloned.1.call-update) | async-done | bytes 32784 | tf_op jit(solution)/shard_map/reduce_scatter | solution.py:24
  314.6 75.0 %reduce-scatter.15.cloned.1.call-done = f32[64,128]{1,0:T(8,128)} async-done(((f32[64,2048]{1,0:T(8,128)}), f32[64,128]{1,0:T(8,128)}) %reduce-scatter.15.cloned.1.call-update) | async-done | bytes 32784 | tf_op jit(solution)/shard_map/reduce_scatter | solution.py:67
  389.6 0.8 multiply_add_fusion.2
  390.4 0.2 fusion.61
  390.6 85.2 %psum.29 = f32[64,64]{0,1:T(8,128)S(1)} all-reduce(f32[64,64]{0,1:T(8,128)S(1)} %fusion.61), channel_id=1, replica_groups=mesh['row'=16,'col'=16] {'row','col'}, use_global_device_ids=true, to_apply=%region_7.10 | all-reduce | flops 4096 | bytes 32768 | tf_op jit(solution)/shard_map/psum | solution.py:18
  475.7 0.1 copy.24
  475.8 5.8 cholesky.85
  481.7 0.6 compare_reduce_fusion.2
  482.3 0.7 fusion.2
  483.0 4.9 custom-call.11
  487.9 0.3 multiply_convert_fusion.1
  488.2 34.1 %all_gather.20 = bf16[64,2048]{1,0:T(8,128)(2,1)S(1)} all-gather(bf16[64,128]{1,0:T(8,128)(2,1)S(1)} %get-tuple-element.9), channel_id=1, replica_groups=mesh['row'=16,'col'=16] {'row'}, dimensions={1}, use_global_device_ids=true | all-gather | bytes 278528 | tf_op jit(solution)/shard_map/all_gather | solution.py:29
  522.3 6.9 fusion.62
  529.2 36.1 %all_gather.21 = bf16[64,2048]{1,0:T(8,128)(2,1)S(1)} all-gather(bf16[64,128]{1,0:T(8,128)(2,1)S(1)} %get-tuple-element.9), channel_id=1, replica_groups=mesh['row'=16,'col'=16] {'col'}, dimensions={1}, use_global_device_ids=true | all-gather | bytes 278528 | tf_op jit(solution)/shard_map/all_gather | solution.py:86
  565.3 5.8 fusion.63
  571.2 35.5 %reduce-scatter.17.cloned.1.call-done = f32[64,128]{1,0:T(8,128)} async-done(((f32[64,2048]{1,0:T(8,128)}), f32[64,128]{1,0:T(8,128)}) %reduce-scatter.17.cloned.1.call-update) | async-done | bytes 32784 | tf_op jit(solution)/shard_map/reduce_scatter | solution.py:24
  606.7 74.7 %reduce-scatter.19.cloned.1.call-done = f32[64,128]{1,0:T(8,128)} async-done(((f32[64,2048]{1,0:T(8,128)}), f32[64,128]{1,0:T(8,128)}) %reduce-scatter.19.cloned.1.call-update) | async-done | bytes 32784 | tf_op jit(solution)/shard_map/reduce_scatter | solution.py:67
  681.4 0.8 multiply_add_fusion.1
  682.2 0.2 fusion.64
  682.4 85.6 %psum.30 = f32[64,64]{0,1:T(8,128)S(1)} all-reduce(f32[64,64]{0,1:T(8,128)S(1)} %fusion.64), channel_id=1, replica_groups=mesh['row'=16,'col'=16] {'row','col'}, use_global_device_ids=true, to_apply=%region_10.13 | all-reduce | flops 4096 | bytes 32768 | tf_op jit(solution)/shard_map/psum | solution.py:18
  768.0 0.1 copy.26
  768.1 5.8 cholesky.96
  774.0 0.6 compare_reduce_fusion.1
  774.6 0.7 fusion.3
  775.3 4.9 custom-call.12
  780.2 0.3 multiply_convert_fusion
  780.4 34.1 %all_gather.22 = bf16[64,2048]{1,0:T(8,128)(2,1)S(1)} all-gather(bf16[64,128]{1,0:T(8,128)(2,1)S(1)} %get-tuple-element.11), channel_id=1, replica_groups=mesh['row'=16,'col'=16] {'row'}, dimensions={1}, use_global_device_ids=true | all-gather | bytes 278528 | tf_op jit(solution)/shard_map/all_gather | solution.py:29
  814.5 6.9 fusion.65
  821.5 35.9 %all_gather.23 = bf16[64,2048]{1,0:T(8,128)(2,1)S(1)} all-gather(bf16[64,128]{1,0:T(8,128)(2,1)S(1)} %get-tuple-element.11), channel_id=1, replica_groups=mesh['row'=16,'col'=16] {'col'}, dimensions={1}, use_global_device_ids=true | all-gather | bytes 278528 | tf_op jit(solution)/shard_map/all_gather | solution.py:86
  857.4 5.8 fusion.66
  863.2 35.7 %reduce-scatter.21.cloned.1.call-done = f32[64,128]{1,0:T(8,128)} async-done(((f32[64,2048]{1,0:T(8,128)}), f32[64,128]{1,0:T(8,128)}) %reduce-scatter.21.cloned.1.call-update) | async-done | bytes 32784 | tf_op jit(solution)/shard_map/reduce_scatter | solution.py:24
  899.0 75.8 %reduce-scatter.23.cloned.1.call-done = f32[64,128]{1,0:T(8,128)} async-done(((f32[64,2048]{1,0:T(8,128)}), f32[64,128]{1,0:T(8,128)}) %reduce-scatter.23.cloned.1.call-update) | async-done | bytes 32784 | tf_op jit(solution)/shard_map/reduce_scatter | solution.py:67
  974.7 0.8 multiply_add_fusion
  975.5 0.2 fusion.67
  975.7 84.6 %psum.31 = f32[64,64]{0,1:T(8,128)S(1)} all-reduce(f32[64,64]{0,1:T(8,128)S(1)} %fusion.67), channel_id=1, replica_groups=mesh['row'=16,'col'=16] {'row','col'}, use_global_device_ids=true, to_apply=%region_13.16 | all-reduce | flops 4096 | bytes 32768 | tf_op jit(solution)/shard_map/psum | solution.py:18
  1060.3 0.1 copy.28
  1060.4 5.8 cholesky.107
  1066.3 0.6 compare_reduce_fusion
  1066.9 0.7 fusion.4
  1067.6 4.9 custom-call.13
  1072.5 0.9 convolution_multiply_fusion
  (36 shorter events, 0.7 us)
Async XLA Ops:
  6.5 24.3 %copy-start = (f32[64,128]{1,0:T(8,128)S(1)}, f32[64,128]{1,0:T(8,128)}, u32[]{:S(2)}) copy-start(f32[64,128]{1,0:T(8,128)} %param.7) | copy-start | bytes 98308
  6.5 170.2 %reduce-scatter.25.cloned.1.call-start = ((), (), s32[]{:S(2)}) async-start(), calls=%async_computation.14 | async-start | bytes 1114112
  16.3 3.2 copy-start.1
  22.9 7.9 copy-start.2
  22.9 159.6 %reduce-scatter.27.cloned.1.call-start = ((), (), s32[]{:S(2)}) async-start(), calls=%async_computation.15 | async-start | bytes 1114112
  30.7 283.8 %reduce-scatter.13.cloned.1.call-start = ((), (), s32[]{:S(2)}) async-start(), calls=%async_computation.8 | async-start | bytes 557056 | tf_op jit(solution)/shard_map/reduce_scatter | solution.py:24
  223.1 166.5 %reduce-scatter.15.cloned.1.call-start = ((), (), s32[]{:S(2)}) async-start(), calls=%async_computation.9 | async-start | bytes 557056 | tf_op jit(solution)/shard_map/reduce_scatter | solution.py:67
  279.3 327.4 %reduce-scatter.17.cloned.1.call-start = ((), (), s32[]{:S(2)}) async-start(), calls=%async_computation.10 | async-start | bytes 557056 | tf_op jit(solution)/shard_map/reduce_scatter | solution.py:24
  529.2 152.2 %reduce-scatter.19.cloned.1.call-start = ((), (), s32[]{:S(2)}) async-start(), calls=%async_computation.11 | async-start | bytes 557056 | tf_op jit(solution)/shard_map/reduce_scatter | solution.py:67
  571.1 327.8 %reduce-scatter.21.cloned.1.call-start = ((), (), s32[]{:S(2)}) async-start(), calls=%async_computation.12 | async-start | bytes 557056 | tf_op jit(solution)/shard_map/reduce_scatter | solution.py:24
  821.4 153.3 %reduce-scatter.23.cloned.1.call-start = ((), (), s32[]{:S(2)}) async-start(), calls=%async_computation.13 | async-start | bytes 557056 | tf_op jit(solution)/shard_map/reduce_scatter | solution.py:67
Sparse Core Ops, SparseCore 0:
  23.1 81.6 reduce-scatter.24
  107.3 75.2 reduce-scatter.26
  223.2 91.2 reduce-scatter.12
  316.9 72.6 reduce-scatter.14
  529.3 77.3 reduce-scatter.16
  609.1 72.2 reduce-scatter.18
  821.5 77.3 reduce-scatter.20
  901.4 73.2 reduce-scatter.22
where the time goes:
time: 1080 us
  blocking collectives  561 us (52%)
  waiting for transfers between devices  337 us (31%)
  other arithmetic  59.2 us (5%)
  local copies, waits for them, and re-layouts  57.1 us (5%)
  matrix products  51.7 us (5%)
  between operations  13.8 us (1%)
    psum x4, blocking collectives, orthonormalize(): total_gram = lax.psum(partial_gram, ('row', 'col'))  338 us
    reduce_scatter x3, waiting for transfers between devices, mirror_sums(): return lax.psum_scatter(term, 'row', scatter_dimension=1, tiled=True)  225 us
    all_gather x3, blocking collectives, local(): lax.all_gather(vectors, 'col', axis=1, tiled=True)  122 us
    reduce_scatter x3, waiting for transfers between devices, collect_direct(): return lax.psum_scatter(term, 'col', scatter_dimension=1, tiled=True)  106 us
    all_gather x3, blocking collectives, direct_part(): lax.all_gather(vectors, 'row', axis=1, tiled=True)  101 us
    gather x1, local copies, waits for them, and re-layouts, local(): jnp.take_along_axis(start_vectors, jnp.broadcast_to(cluster_order, start_...  50.7 us
    another operation x12, other arithmetic, orthonormalize(): factor = jnp.linalg.cholesky(total_gram)  26.1 us
    another operation x8, other arithmetic, orthonormalize(): return jax.scipy.linalg.solve_triangular(factor, panel_in, lower=True)  22.2 us
  transfers between devices with their start and end apart: 8, of which 7 were waited for; matrix products, arithmetic and copies ran while one was open for 8% of the time, Pallas kernels for 0%

commit v1 on v0

--- a/solution.py
+++ b/solution.py
@@ -15,7 +15,7 @@
         precision=lax.Precision.HIGHEST,
         preferred_element_type=jnp.float32,
     )
-    total_gram = lax.psum(partial_gram, ("row", "col"))
+    total_gram = jnp.sum(jax.lax.all_gather(partial_gram, ("row", "col")), axis=0)
     factor = jnp.linalg.cholesky(total_gram)
     return jax.scipy.linalg.solve_triangular(factor, panel_in, lower=True)
 

time: 1080 us -> 2450 us (2.27)
  waiting for transfers between devices: 337 us -> 2030 us
  blocking collectives: 561 us -> 213 us
    all_gather x0 -> x4, waiting for transfers between devices: none -> 1600 us  [orthonormalize(): jax.lax.all_gather(partial_gram, ('row', 'col'))]
    psum x4 -> x0, blocking collectives: 338 us -> none  [orthonormalize(): total_gram = lax.psum(partial_gram, ('row', 'col'))]
    unnamed x10 -> x14, waiting for transfers between devices: 5.01 us -> 98.3 us
  transfers between devices with their start and end apart: 8 -> 12, of which waited for: 7 -> 12; matrix products, arithmetic and copies ran while one was open for 8% -> 3% of each run, Pallas kernels for 0% -> 0%
where the time goes in v1:
time: 2450 us
  waiting for transfers between devices  2030 us (83%)
  blocking collectives  213 us (9%)
  other arithmetic  75.2 us (3%)
  local copies, waits for them, and re-layouts  57.2 us (2%)
  matrix products  54.1 us (2%)
    all_gather x4, waiting for transfers between devices, orthonormalize(): jax.lax.all_gather(partial_gram, ('row', 'col'))  1600 us
    reduce_scatter x3, waiting for transfers between devices, mirror_sums(): return lax.psum_scatter(term, 'row', scatter_dimension=1, tiled=True)  225 us
    all_gather x3, blocking collectives, local(): lax.all_gather(vectors, 'col', axis=1, tiled=True)  114 us
    reduce_scatter x3, waiting for transfers between devices, collect_direct(): return lax.psum_scatter(term, 'col', scatter_dimension=1, tiled=True)  109 us
    all_gather x3, blocking collectives, direct_part(): lax.all_gather(vectors, 'row', axis=1, tiled=True)  99.4 us
    unnamed x14, waiting for transfers between devices  98.3 us
    gather x1, local copies, waits for them, and re-layouts, local(): jnp.take_along_axis(start_vectors, jnp.broadcast_to(cluster_order, start_...  50.7 us
  transfers between devices with their start and end apart: 12, of which 12 were waited for; matrix products, arithmetic and copies ran while one was open for 3% of the time, Pallas kernels for 0%

profile of v1, /device:TPU:1, one launch (start us, length us, event | category | flops | bytes accessed | tf_op | source)
XLA Modules:
  0.0 2448.8 jit_solution(16080691237863748192)
XLA Ops:
  7.4 0.7 broadcast_compare_fusion
  8.2 1.1 and.66
  9.4 7.7 fusion
  17.1 3.2 copy-done.1
  20.3 3.4 convolution_bitcast_fusion.1
  23.8 7.8 convolution_bitcast_fusion
  31.7 50.7 %gather_fusion = f32[8192]{0:T(1024)S(1)} fusion(f32[64,128]{1,0:T(8,128)S(1)} %copy-done, s32[8192]{0:T(1024)S(1)} %or_bitcast_fusion), kind=kCustom, calls=%fused_computation | custom fusion | bytes 131072 | tf_op jit(solution)/shard_map/jit(take_along_axis)/gather | solution.py:73
  82.4 0.8 fusion.16
  83.4 22.1 reduce-scatter.25.cloned.1.call-done
  105.5 0.9 copy.18
  106.4 76.1 %reduce-scatter.27.cloned.1.call-done = f32[128,1]{1,0:T(8,128)} async-done(((f32[2048,1]{1,0:T(8,128)}), f32[128,1]{1,0:T(8,128)}) %reduce-scatter.27.cloned.1.call-update) | async-done | bytes 528
  182.5 0.9 copy.20
  183.4 322.2 %all-gather.9.cloned.1.call-done = f32[16384,64]{1,0:T(8,128)} async-done(((f32[64,64]{1,0:T(8,128)}), f32[16384,64]{1,0:T(8,128)}) %all-gather.9.cloned.1.call-update) | async-done | bytes 4194320 | tf_op jit(solution)/shard_map/all_gather | solution.py:18
  505.6 4.0 reduce_sum.36
  509.7 5.8 cholesky.74
  515.6 0.6 compare_reduce_fusion.3
  516.2 0.7 fusion.1
  516.9 4.9 custom-call.10
  521.8 0.3 multiply_convert_fusion.2
  522.1 33.3 %all_gather.44 = bf16[64,2048]{1,0:T(8,128)(2,1)S(1)} all-gather(bf16[64,128]{1,0:T(8,128)(2,1)S(1)} %get-tuple-element.6), channel_id=1, replica_groups=mesh['row'=16,'col'=16] {'row'}, dimensions={1}, use_global_device_ids=true | all-gather | bytes 278528 | tf_op jit(solution)/shard_map/all_gather | solution.py:29
  555.3 6.9 fusion.59
  562.3 37.7 %all_gather.45 = bf16[64,2048]{1,0:T(8,128)(2,1)S(1)} all-gather(bf16[64,128]{1,0:T(8,128)(2,1)S(1)} %get-tuple-element.6), channel_id=1, replica_groups=mesh['row'=16,'col'=16] {'col'}, dimensions={1}, use_global_device_ids=true | all-gather | bytes 278528 | tf_op jit(solution)/shard_map/all_gather | solution.py:86
  599.9 5.8 fusion.60
  605.8 36.3 %reduce-scatter.13.cloned.1.call-done = f32[64,128]{1,0:T(8,128)} async-done(((f32[64,2048]{1,0:T(8,128)}), f32[64,128]{1,0:T(8,128)}) %reduce-scatter.13.cloned.1.call-update) | async-done | bytes 32784 | tf_op jit(solution)/shard_map/reduce_scatter | solution.py:24
  642.2 75.6 %reduce-scatter.15.cloned.1.call-done = f32[64,128]{1,0:T(8,128)} async-done(((f32[64,2048]{1,0:T(8,128)}), f32[64,128]{1,0:T(8,128)}) %reduce-scatter.15.cloned.1.call-update) | async-done | bytes 32784 | tf_op jit(solution)/shard_map/reduce_scatter | solution.py:67
  717.8 0.8 multiply_add_fusion.2
  718.6 0.8 fusion.61
  719.5 425.6 %all-gather.11.cloned.1.call-done = f32[16384,64]{1,0:T(8,128)} async-done(((f32[64,64]{1,0:T(8,128)}), f32[16384,64]{1,0:T(8,128)}) %all-gather.11.cloned.1.call-update) | async-done | bytes 4194320 | tf_op jit(solution)/shard_map/all_gather | solution.py:18
  1145.1 4.0 reduce_sum.37
  1149.2 5.8 cholesky.85
  1155.1 0.6 compare_reduce_fusion.2
  1155.7 0.7 fusion.2
  1156.4 4.9 custom-call.11
  1161.3 0.3 multiply_convert_fusion.1
  1161.5 33.1 %all_gather.48 = bf16[64,2048]{1,0:T(8,128)(2,1)S(1)} all-gather(bf16[64,128]{1,0:T(8,128)(2,1)S(1)} %get-tuple-element.9), channel_id=1, replica_groups=mesh['row'=16,'col'=16] {'row'}, dimensions={1}, use_global_device_ids=true | all-gather | bytes 278528 | tf_op jit(solution)/shard_map/all_gather | solution.py:29
  1194.6 6.9 fusion.62
  1201.6 38.0 %all_gather.49 = bf16[64,2048]{1,0:T(8,128)(2,1)S(1)} all-gather(bf16[64,128]{1,0:T(8,128)(2,1)S(1)} %get-tuple-element.9), channel_id=1, replica_groups=mesh['row'=16,'col'=16] {'col'}, dimensions={1}, use_global_device_ids=true | all-gather | bytes 278528 | tf_op jit(solution)/shard_map/all_gather | solution.py:86
  1239.6 5.8 fusion.63
  1245.5 36.1 %reduce-scatter.17.cloned.1.call-done = f32[64,128]{1,0:T(8,128)} async-done(((f32[64,2048]{1,0:T(8,128)}), f32[64,128]{1,0:T(8,128)}) %reduce-scatter.17.cloned.1.call-update) | async-done | bytes 32784 | tf_op jit(solution)/shard_map/reduce_scatter | solution.py:24
  1281.6 74.7 %reduce-scatter.19.cloned.1.call-done = f32[64,128]{1,0:T(8,128)} async-done(((f32[64,2048]{1,0:T(8,128)}), f32[64,128]{1,0:T(8,128)}) %reduce-scatter.19.cloned.1.call-update) | async-done | bytes 32784 | tf_op jit(solution)/shard_map/reduce_scatter | solution.py:67
  1356.4 0.8 multiply_add_fusion.1
  1357.2 0.8 fusion.64
  1358.0 426.6 %all-gather.13.cloned.1.call-done = f32[16384,64]{1,0:T(8,128)} async-done(((f32[64,64]{1,0:T(8,128)}), f32[16384,64]{1,0:T(8,128)}) %all-gather.13.cloned.1.call-update) | async-done | bytes 4194320 | tf_op jit(solution)/shard_map/all_gather | solution.py:18
  1784.6 4.0 reduce_sum.38
  1788.7 5.8 cholesky.96
  1794.6 0.6 compare_reduce_fusion.1
  1795.2 0.7 fusion.3
  1795.9 4.9 custom-call.12
  1800.8 0.3 multiply_convert_fusion
  1801.0 33.1 %all_gather.52 = bf16[64,2048]{1,0:T(8,128)(2,1)S(1)} all-gather(bf16[64,128]{1,0:T(8,128)(2,1)S(1)} %get-tuple-element.11), channel_id=1, replica_groups=mesh['row'=16,'col'=16] {'row'}, dimensions={1}, use_global_device_ids=true | all-gather | bytes 278528 | tf_op jit(solution)/shard_map/all_gather | solution.py:29
  1834.1 6.9 fusion.65
  1841.1 37.8 %all_gather.53 = bf16[64,2048]{1,0:T(8,128)(2,1)S(1)} all-gather(bf16[64,128]{1,0:T(8,128)(2,1)S(1)} %get-tuple-element.11), channel_id=1, replica_groups=mesh['row'=16,'col'=16] {'col'}, dimensions={1}, use_global_device_ids=true | all-gather | bytes 278528 | tf_op jit(solution)/shard_map/all_gather | solution.py:86
  1878.9 5.8 fusion.66
  1884.8 36.3 %reduce-scatter.21.cloned.1.call-done = f32[64,128]{1,0:T(8,128)} async-done(((f32[64,2048]{1,0:T(8,128)}), f32[64,128]{1,0:T(8,128)}) %reduce-scatter.21.cloned.1.call-update) | async-done | bytes 32784 | tf_op jit(solution)/shard_map/reduce_scatter | solution.py:24
  1921.1 74.9 %reduce-scatter.23.cloned.1.call-done = f32[64,128]{1,0:T(8,128)} async-done(((f32[64,2048]{1,0:T(8,128)}), f32[64,128]{1,0:T(8,128)}) %reduce-scatter.23.cloned.1.call-update) | async-done | bytes 32784 | tf_op jit(solution)/shard_map/reduce_scatter | solution.py:67
  1996.0 0.8 multiply_add_fusion
  1996.8 0.8 fusion.67
  1997.6 426.5 %all-gather.15.cloned.1.call-done = f32[16384,64]{1,0:T(8,128)} async-done(((f32[64,64]{1,0:T(8,128)}), f32[16384,64]{1,0:T(8,128)}) %all-gather.15.cloned.1.call-update) | async-done | bytes 4194320 | tf_op jit(solution)/shard_map/all_gather | solution.py:18
  2424.1 4.0 reduce_sum.39
  2428.2 5.8 cholesky.107
  2434.1 0.6 compare_reduce_fusion
  2434.7 0.7 fusion.4
  2435.4 4.9 custom-call.13
  2440.3 0.9 convolution_multiply_fusion
  (48 shorter events, 1.4 us)
Async XLA Ops:
  7.4 24.3 copy-start
  7.4 98.1 %reduce-scatter.25.cloned.1.call-start = ((), (), s32[]{:S(2)}) async-start(), calls=%async_computation.18 | async-start | bytes 1114112
  17.1 3.2 copy-start.1
  23.7 7.9 copy-start.2
  23.7 158.7 %reduce-scatter.27.cloned.1.call-start = ((), (), s32[]{:S(2)}) async-start(), calls=%async_computation.19 | async-start | bytes 1114112
  31.6 474.0 %all-gather.9.cloned.1.call-start = ((), (), s32[]{:S(2)}) async-start(), calls=%async_computation.14 | async-start | bytes 8421376 | tf_op jit(solution)/shard_map/all_gather | solution.py:18
  83.2 559.0 %reduce-scatter.13.cloned.1.call-start = ((), (), s32[]{:S(2)}) async-start(), calls=%async_computation.8 | async-start | bytes 557056 | tf_op jit(solution)/shard_map/reduce_scatter | solution.py:24
  562.2 155.6 %reduce-scatter.15.cloned.1.call-start = ((), (), s32[]{:S(2)}) async-start(), calls=%async_computation.9 | async-start | bytes 557056 | tf_op jit(solution)/shard_map/reduce_scatter | solution.py:67
  605.8 539.3 %all-gather.11.cloned.1.call-start = ((), (), s32[]{:S(2)}) async-start(), calls=%async_computation.15 | async-start | bytes 8421376 | tf_op jit(solution)/shard_map/all_gather | solution.py:18
  719.4 562.2 %reduce-scatter.17.cloned.1.call-start = ((), (), s32[]{:S(2)}) async-start(), calls=%async_computation.10 | async-start | bytes 557056 | tf_op jit(solution)/shard_map/reduce_scatter | solution.py:24
  1201.5 154.8 %reduce-scatter.19.cloned.1.call-start = ((), (), s32[]{:S(2)}) async-start(), calls=%async_computation.11 | async-start | bytes 557056 | tf_op jit(solution)/shard_map/reduce_scatter | solution.py:67
  1245.5 539.1 %all-gather.13.cloned.1.call-start = ((), (), s32[]{:S(2)}) async-start(), calls=%async_computation.16 | async-start | bytes 8421376 | tf_op jit(solution)/shard_map/all_gather | solution.py:18
  1358.0 563.1 %reduce-scatter.21.cloned.1.call-start = ((), (), s32[]{:S(2)}) async-start(), calls=%async_computation.12 | async-start | bytes 557056 | tf_op jit(solution)/shard_map/reduce_scatter | solution.py:24
  1841.0 155.0 %reduce-scatter.23.cloned.1.call-start = ((), (), s32[]{:S(2)}) async-start(), calls=%async_computation.13 | async-start | bytes 557056 | tf_op jit(solution)/shard_map/reduce_scatter | solution.py:67
  1884.7 539.4 %all-gather.15.cloned.1.call-start = ((), (), s32[]{:S(2)}) async-start(), calls=%async_computation.17 | async-start | bytes 8421376 | tf_op jit(solution)/shard_map/all_gather | solution.py:18
Sparse Core Ops, SparseCore 0:
  23.8 81.6 reduce-scatter.24
  108.0 74.4 reduce-scatter.26
  562.4 79.7 reduce-scatter.12
  644.5 73.2 reduce-scatter.14
  1201.6 79.9 reduce-scatter.16
  1284.0 72.3 reduce-scatter.18
  1841.1 79.9 reduce-scatter.20
  1923.6 72.3 reduce-scatter.22
Sparse Core Ops, SparseCore 1:
  83.3 422.3 all-gather.8
  719.5 425.5 all-gather.10
  1358.1 426.5 all-gather.12
  1997.7 426.4 all-gather.14
